TPU v7x, 32 devices: a whole 2x2x4 slice. The times are simulated.
32 devices in a mesh: bins: 16 (over z, y, x), diag: 2 (over core).
Axes of the slice: x: 2, y: 2, z: 4, core: 2. Of those that a mesh axis runs over, the one named last changes fastest.
Arguments:
- held_tiles: float32 [32, 2, 1024, 1024], P('bins', 'diag'), may hold values from 0.01 to 20, as said below
- placed: int32 [32], P('bins'), may hold values from 0 to 1, as said below
- bin_mask: int32 [32768], P('bins'), may hold values 0 or 1
- bias: float32 [32768], P('bins'), may hold values from 0.5 to 2
Outputs:
- balanced: float32 [32, 2, 1024, 1024], P('bins', 'diag')
- bias_out: float32 [32768], P('bins')
Inputs may be any that keep to these rules, and one draw needn't show every extreme that they name: placed[q] equals placed[(q + 16) mod 32]; placed[q] is 1 where q is a multiple of 2. `held_tiles`: entries are positive.
All inputs are finite; a program needn't handle non-finite values. No bound on the sum of `bin_mask` on one device may be relied on, other than what follows from the above.
Results may differ from a plain program's by a relative error of at most 0.00012.
Values sent between devices are 32-bit elements; how exact they have to be, the bound alone decides.
A program may use at most 128 MiB of HBM per device.

v0:
```python
import jax
import jax.numpy as jnp
from jax import lax
from jax.sharding import PartitionSpec as P

ITERS = 2


def passed_along(value, axis, steps):
    count = lax.axis_size(axis)
    first, last = (max(0, -steps), min(count, count - steps))
    return lax.ppermute(value, axis, [(source, source + steps) for source in range(first, last)])


def partner(value, axis, stride):
    mask = 2**stride
    pairs = [(source, source ^ mask) for source in range(lax.axis_size(axis))]
    return lax.ppermute(value, axis, pairs)


def local(held_tiles, placed, bin_mask, bias):
    rows_dev = held_tiles.shape[0]
    tile_size = held_tiles.shape[2]
    offset_index = lax.axis_index("diag")
    on_diagonal = offset_index == 0
    top_bit = lax.axis_size("bins").bit_length() - 2
    held_local = held_tiles[:, 0]
    placed_flags = (placed == 1)[:, None]
    live_home = bin_mask.astype(jnp.float32).reshape(rows_dev, tile_size)
    first_next = passed_along(live_home[0:1], "bins", -1)
    live_next = jnp.concatenate([live_home[1:], first_next], axis=0)
    lines = jnp.arange(tile_size, dtype=jnp.int32)
    upper_mask = (lines[:, None] <= lines[None, :]).astype(jnp.float32)
    triangle = jnp.where(on_diagonal, upper_mask, 1.0)
    partner_tiles = partner(held_local, "bins", top_bit)
    home_tiles = jnp.where(placed_flags[:, :, None], partner_tiles, held_local)
    live_cols = jnp.where(on_diagonal, live_home, live_next)
    scaled = home_tiles * triangle * live_home[:, :, None] * live_cols[:, None, :]
    bias_now = bias.reshape(rows_dev, tile_size)
    for repeat in range(ITERS):
        row_part = jnp.sum(scaled, axis=2)
        diagonal_terms = jnp.diagonal(scaled, axis1=1, axis2=2)
        col_part = jnp.sum(scaled, axis=1) - jnp.where(on_diagonal, diagonal_terms, 0.0)
        edge_cols = passed_along(col_part[-1:], "bins", 1)
        moved_cols = jnp.concatenate([edge_cols, col_part[:-1]], axis=0)
        contrib = row_part + jnp.where(on_diagonal, col_part, moved_cols)
        sums = lax.psum(contrib, "diag")
        masked_total, live_count = lax.psum((jnp.sum(sums * live_home), jnp.sum(live_home)), "bins")
        mean_sum = masked_total / live_count
        factor = jnp.where(live_home > 0, sums / mean_sum, 1.0)
        bias_now = bias_now * factor
        inverse = 1.0 / factor
        inverse_first = passed_along(inverse[0:1], "bins", -1)
        inverse_next = jnp.concatenate([inverse[1:], inverse_first], axis=0)
        inverse_cols = jnp.where(on_diagonal, inverse, inverse_next)
        scaled = scaled * inverse[:, :, None] * inverse_cols[:, None, :]
    return (scaled[:, None], bias_now.reshape(rows_dev * tile_size))


def solution(mesh):
    placed = (P("bins", "diag", None, None), P("bins"), P("bins"), P("bins"))
    return jax.shard_map(
        local,
        mesh=mesh,
        in_specs=placed,
        out_specs=(P("bins", "diag", None, None), P("bins")),
        check_vma=False,
    )
```

profile of v0, /device:TPU:0, one launch (start us, length us, event | category | flops | bytes accessed | tf_op | source)
XLA Modules:
  0.0 558.6 jit_solution(11005354058122604482)
XLA Ops:
  0.6 15.4 %copy.29 = f32[2,1,1024,1024]{3,0,2,1:T(2,128)} copy(f32[2,1,1024,1024]{3,2,1,0:T(8,128)} %param.4) | data formatting | bytes 16777216 | tf_op args[0]
  16.0 4.1 collective-permute-start
  20.1 1.3 collective-permute-start.1
  21.4 2.5 convert_select_fusion
  24.1 1.4 collective-permute-done.1
  25.6 355.1 %collective-permute-done = f32[2,1024,1024]{2,0,1:T(2,128)} collective-permute-done((f32[2,1024,1024]{2,0,1:T(2,128)}, f32[2,1024,1024]{2,0,1:T(2,128)}, u32[]{:S(2)}, u32[]{:S(2)}) %collective-permute-start) | collective-permute-done | bytes 8388640 | tf_op jit(solution)/shard_map/ppermute | solution.py:18
  380.7 19.2 %fusion.3 = (f32[2,1024]{1,0:T(2,128)S(1)}, f32[2,1024]{0,1:T(8,128)S(1)}, f32[2,1024,1024]{2,0,1:T(2,128)}) fusion(f32[2,1024]{1,0:T(2,128)S(1)} %maximum_select_fusion, f32[2,1024]{0,1:T(8,128)S(1)} %copy.17, f32[1024,1024]{1,0:T(8,128)} %convert_select_fusion, f32[2,1024,1024]{2,0,1:T(2,128)} %collective-permute-done, f32[2,1,1024,1024]{3,2,1,0:T(8,128)} %param.4, ...), kind=kLoop, calls=%fused_computation.30 | loop fusion | flops 12578816 | bytes 29392898 | tf_op jit(solution)/shard_map/reduce_sum | solution.py:43
  399.8 13.3 %gather_fusion = f32[1024,2]{0,1:T(2,128)S(1)} fusion(f32[2,1024,1024]{2,0,1:T(2,128)} %get-tuple-element.19, s32[1024]{0:T(1024)S(1)} %bitcast.20), kind=kCustom, calls=%fused_computation | custom fusion | bytes 24576 | tf_op jit(solution)/shard_map/jit(diagonal)/gather | solution.py:42
  413.2 3.4 collective-permute-start.2
  416.6 0.7 convert_reduce_fusion
  417.9 2.5 psum.38
  421.0 43.4 %all-reduce = (f32[]{:T(128)}, f32[]{:T(128)}) all-reduce(f32[]{:T(128)} %multiply_reduce_fusion.1, f32[]{:T(128)} %convert_reduce_fusion), channel_id=1, replica_groups=mesh['bins'=16,'diag'=2] {'bins'}, use_global_device_ids=true, to_apply=%region_4.5 | all-reduce | flops 2 | bytes 16 | tf_op jit(solution)/shard_map/psum | solution.py:48
  465.8 1.3 collective-permute-start.3
  467.4 4.0 collective-permute-done.3
  471.4 9.7 %fusion.2 = (f32[2,1024]{1,0:T(2,128)S(1)}, f32[2,1024]{0,1:T(8,128)S(1)}, f32[2,1024,1024]{2,0,1:T(2,128)}) fusion(f32[2,1024]{1,0:T(2,128)S(1)} %maximum_select_fusion.2, f32[2,1024,1024]{2,0,1:T(2,128)} %get-tuple-element.19, f32[2,1024]{0,1:T(8,128)S(1)} %copy.19), kind=kLoop, calls=%fused_computation.29 | loop fusion | flops 8384512 | bytes 16809984 | tf_op jit(solution)/shard_map/reduce_sum | solution.py:43
  481.0 13.3 %gather_fusion.1 = f32[1024,2]{0,1:T(2,128)S(1)} fusion(f32[2,1024,1024]{2,0,1:T(2,128)} %get-tuple-element.16, s32[1024]{0:T(1024)S(1)} %bitcast.21), kind=kCustom, calls=%fused_computation.1 | custom fusion | bytes 24576 | tf_op jit(solution)/shard_map/jit(diagonal)/gather | solution.py:42
  494.4 1.7 collective-permute-start.4
  496.2 1.1 collective-permute-done.4
  497.4 2.5 psum.41
  500.5 39.5 %psum.42 = f32[]{:T(128)} all-reduce(f32[]{:T(128)} %multiply_reduce_fusion), channel_id=1, replica_groups=mesh['bins'=16,'diag'=2] {'bins'}, use_global_device_ids=true, to_apply=%region_11.12 | all-reduce | flops 1 | bytes 8 | tf_op jit(solution)/shard_map/psum | solution.py:48
  541.4 1.3 collective-permute-start.5
  543.5 3.4 collective-permute-done.5
  546.9 5.7 %multiply_bitcast_fusion = f32[2,1,1024,1024]{3,0,2,1:T(2,128)S(1)} fusion(f32[2,1024,1024]{2,0,1:T(2,128)} %get-tuple-element.16, f32[2,1024]{1,0:T(2,128)S(1)} %maximum_select_fusion.4, f32[2,1024]{0,1:T(8,128)S(1)} %copy.21), kind=kLoop, calls=%fused_computation.3 | loop fusion | flops 4194304 | bytes 16793600 | tf_op jit(solution)/shard_map/broadcast_in_dim | solution.py:57
  552.7 6.0 %copy.22 = f32[2,1,1024,1024]{3,2,1,0:T(8,128)} copy(f32[2,1,1024,1024]{3,0,2,1:T(2,128)S(1)} %multiply_bitcast_fusion) | data formatting | bytes 16777216
  (35 shorter events, 3.5 us)
Async XLA Ops:
  0.6 19.5 %copy-start = (s32[2048]{0:T(1024)S(1)}, s32[2048]{0:T(1024)}, u32[]{:S(2)}) copy-start(s32[2048]{0:T(1024)} %param.6) | copy-start | bytes 24580
  0.6 23.2 %copy-start.2 = (s32[2]{0:T(128)S(1)}, s32[2]{0:T(128)}, u32[]{:S(2)}) copy-start(s32[2]{0:T(128)} %param.5) | copy-start | bytes 28
  16.0 364.6 %collective-permute-start = (f32[2,1024,1024]{2,0,1:T(2,128)}, f32[2,1024,1024]{2,0,1:T(2,128)}, u32[]{:S(2)}, u32[]{:S(2)}) collective-permute-start(f32[2,1024,1024]{2,0,1:T(2,128)} %bitcast.18), channel_id=1, source_target_pairs={{0,16},{2,18},{4,20},{6,22},{8,24},{10,26},{12,28},{14,30},{16,0},... | collective-permute-start | bytes 25165832 | tf_op jit(solution)/shard_map/ppermute | solution.py:18
  20.1 5.5 collective-permute-start.1
  413.2 4.7 collective-permute-start.2
  465.8 5.5 collective-permute-start.3
  471.4 29.1 %copy-start.1 = (f32[2048]{0:T(1024)S(1)}, f32[2048]{0:T(1024)}, u32[]{:S(2)}) copy-start(f32[2048]{0:T(1024)} %param.7) | copy-start | bytes 24580
  494.4 3.0 collective-permute-start.4
  541.4 5.5 collective-permute-start.5
where the time goes:
time: 560 us; the launch traced here: 559 us
  waiting for transfers between devices  365 us (65%)
  blocking collectives  87.9 us (16%)
  local copies, waits for them, and re-layouts  49.6 us (9%)
  other arithmetic  39.1 us (7%)
  starting transfers between devices  13 us (2%)
    ppermute x1, waiting for transfers between devices, partner(): return lax.ppermute(value, axis, pairs)  355 us
    psum x2, blocking collectives, local(): lax.psum((jnp.sum(sums * live_home), jnp.sum(live_home)), 'bins')  82.9 us
    reduce_sum x2, other arithmetic, local(): jnp.sum(scaled, axis=1) - jnp.where(on_diagonal, diagonal_terms, 0.0)  28.8 us
    gather x2, local copies, waits for them, and re-layouts, local(): diagonal_terms = jnp.diagonal(scaled, axis1=1, axis2=2)  26.6 us
    unnamed x9, local copies, waits for them, and re-layouts  22 us
  transfers between devices with their start and end apart: 6, of which 6 were waited for; matrix products, arithmetic and copies ran while one was open for 1% of the time, Pallas kernels for 0%

commit v1 on v0

v1 whole, which is shorter than its diff:
```python
import functools

import jax
import jax.numpy as jnp
from jax import lax
from jax.experimental import pallas as pl
from jax.experimental.pallas import tpu as pltpu
from jax.sharding import PartitionSpec as P

ITERS = 2
B = 128
MESH = pl.DeviceIdType.MESH
F32 = jnp.float32


def kernel(n, rows_dev, size, held, placed, mask, bias, tiles_out, u_out, v_out, bias_out,
           home, recv, live_col, next_mask, row, col_acc, diag_vec, contrib, pair, edge_in, edge_out, nxt, tot,
           in_sem, out_sem, send_sem, recv_sem, mask_sem, pair_sem, edge_sem, next_sem, tot_sem):
    b, d = lax.axis_index("bins"), lax.axis_index("diag")
    count = n * 2
    me = b * 2 + d
    on_diag, off_diag = d == 0, d == 1
    has_prev, has_next = b > 0, b < n - 1
    strips = size // B
    width = rows_dev * size
    half = n // 2
    partner = (lax.rem(b + half, n), d)

    barrier = pltpu.get_barrier_semaphore()

    def other(off):
        target = lax.rem(me + off, count)
        return (target // 2, lax.rem(target, 2))

    def greet(off, carry):
        pl.semaphore_signal(barrier, inc=1, device_id=other(off), device_id_type=MESH)
        return carry

    lax.fori_loop(1, count, greet, 0)
    loads = []
    for t in range(rows_dev):
        loads.append(pltpu.make_async_copy(held.at[t, 0], home.at[t], in_sem.at[t]))
        loads[-1].start()
    pl.semaphore_wait(barrier, count - 1)

    mask_send = pltpu.make_async_remote_copy(
        mask.at[:, :size], next_mask, mask_sem.at[0], mask_sem.at[1], device_id=(jnp.maximum(b - 1, 0), 1), device_id_type=MESH)

    @pl.when(on_diag & has_prev)
    def _():
        mask_send.start()

    def piece(t, r, first):
        part = (t, pl.ds(r * B, B), pl.ds(first, size - first))
        return pltpu.make_async_remote_copy(
            held.at[t, 0, part[1], part[2]], recv.at[part], send_sem.at[t, r], recv_sem.at[t, r],
            device_id=partner, device_id_type=MESH)

    order = [(t, r) for t in range(rows_dev) for r in range(strips)]

    @pl.when(on_diag)
    def _():
        for t, r in order:
            piece(t, r, r * B).start()

    @pl.when(off_diag)
    def _():
        for t, r in order:
            piece(t, r, 0).start()

    @pl.when(off_diag & has_next)
    def _():
        mask_send.wait_recv()

    @pl.when(on_diag & has_prev)
    def _():
        mask_send.wait_send()

    live = mask[...].astype(F32)
    after = jnp.where(has_next, next_mask[...].astype(F32), 0.0)
    live_col[:, width - size:] = jnp.where(on_diag, live[:, width - size:], after)
    if rows_dev > 1:
        live_col[:, :width - size] = jnp.where(on_diag, live[:, :width - size], live[:, size:])
    for t in range(rows_dev):
        loads[t].wait()
    col_acc[...] = jnp.zeros_like(col_acc)
    line = lax.broadcasted_iota(jnp.int32, (B, B), 0)
    lane = lax.broadcasted_iota(jnp.int32, (B, B), 1)
    shift = jnp.where(on_diag, 0, -2 * size)

    def down(vector):
        return jnp.broadcast_to(vector, (B, B)).T

    def folded(block):
        return jnp.sum(block.reshape(B // 8, 8, B), axis=0)

    def lanes(c):
        return pl.ds(pl.multiple_of(c * B, B), B)

    def out_copy(t, r):
        return pltpu.make_async_copy(home.at[t, pl.ds(r * B, B)], tiles_out.at[t, pl.ds(r * B, B)], out_sem.at[t, r])

    for t, r in order:
        @pl.when(on_diag)
        def _():
            piece(t, r, r * B).wait_recv()

        @pl.when(off_diag)
        def _():
            piece(t, r, 0).wait_recv()

        spot = pl.ds(t * size + r * B, B)
        live_down = down(mask[:, spot].astype(F32))
        moved = jnp.broadcast_to(placed[t], (B, B)) == 1

        def first_pass(c, total):
            at = (t, pl.ds(r * B, B), lanes(c))
            block = jnp.where(moved, recv[at], home[at])
            keep = line + (r * B + shift) <= lane + c * B
            across = live_col[:, pl.ds(pl.multiple_of(t * size + c * B, B), B)]
            block = jnp.where(keep, block, 0.0) * live_down * across
            home[at] = block
            col_acc[t, :, lanes(c)] += folded(block)
            return total + block

        total = lax.fori_loop(0, strips, first_pass, jnp.zeros((B, B), F32))
        row[:, spot] = jnp.sum(total.T, axis=0, keepdims=True)
        corner = home[t, pl.ds(r * B, B), pl.ds(r * B, B)]
        corner = jnp.sum(jnp.where(line == lane, corner, 0.0), axis=0, keepdims=True)
        diag_vec[:, spot] = jnp.where(on_diag, corner, 0.0)
        out_copy(t, r).start()

    u_out[...] = jnp.ones_like(u_out)
    v_out[...] = jnp.ones_like(v_out)
    bias_out[...] = bias[...]
    first_lane = lax.broadcasted_iota(jnp.int32, (1, B), 1)

    for k in range(ITERS):
        if k > 0:
            col_acc[...] = jnp.zeros_like(col_acc)
            for t in range(rows_dev):
                def strip_pass(r, carry):
                    spot = pl.ds(pl.multiple_of(t * size + r * B, B), B)
                    u_down = down(u_out[:, spot])

                    def later_pass(c, total):
                        block = home[t, lanes(r), lanes(c)]
                        col_acc[t, :, lanes(c)] += folded(block * u_down)
                        return total + block * v_out[:, pl.ds(pl.multiple_of(t * size + c * B, B), B)]

                    total = lax.fori_loop(0, strips, later_pass, jnp.zeros((B, B), F32))
                    row[:, spot] = jnp.sum(total.T, axis=0, keepdims=True)
                    return carry

                lax.fori_loop(0, strips, strip_pass, 0)
        cols = jnp.concatenate([jnp.sum(col_acc[t], axis=0, keepdims=True) for t in range(rows_dev)], axis=1) * v_out[...]
        rows = row[...] * u_out[...]
        corner = diag_vec[...] * u_out[...] * v_out[...]
        zero = jnp.zeros((1, size), F32)
        moved_cols = jnp.concatenate([zero, cols[:, :width - size]], axis=1)
        mine = rows + jnp.where(on_diag, cols - corner, moved_cols)
        edge = jnp.where(on_diag, 0.0, cols[:, width - size:])
        contrib[k] = mine
        edge_out[k] = edge
        partial = jnp.sum(mine) + jnp.sum(edge)
        kept = jnp.where(on_diag, jnp.sum(mask[...].astype(F32)), 0.0)
        tot[k, me] = jnp.where(first_lane == 0, partial, jnp.where(first_lane == 1, kept, 0.0))

        def tot_copy(off):
            return pltpu.make_async_remote_copy(
                tot.at[k, me], tot.at[k, me], tot_sem.at[k, 0], tot_sem.at[k, 1], device_id=other(off), device_id_type=MESH)

        def tot_start(off, carry):
            tot_copy(off).start()
            return carry

        to_pair = pltpu.make_async_remote_copy(
            contrib.at[k], pair.at[k], pair_sem.at[k, 0], pair_sem.at[k, 1], device_id=(b, 1 - d), device_id_type=MESH)
        to_edge = [pltpu.make_async_remote_copy(
            edge_out.at[k], edge_in.at[k], edge_sem.at[k, i], edge_sem.at[k, 2],
            device_id=(jnp.minimum(b + 1, n - 1), i), device_id_type=MESH) for i in range(2)]
        to_prev = [pltpu.make_async_remote_copy(
            contrib.at[k, :, :size], nxt.at[k, i], next_sem.at[k, 0], next_sem.at[k, 1 + i],
            device_id=(jnp.maximum(b - 1, 0), 1), device_id_type=MESH) for i in range(2)]

        @pl.when(off_diag & has_next)
        def _():
            for copy in to_edge:
                copy.start()

        for i in range(2):
            @pl.when((d == i) & has_prev)
            def _():
                to_prev[i].start()

        lax.fori_loop(1, count, tot_start, 0)
        to_pair.start()
        to_pair.wait()

        @pl.when(off_diag & has_next)
        def _():
            for copy in to_edge:
                copy.wait_send()
            for copy in to_prev:
                copy.wait_recv()

        @pl.when(has_prev)
        def _():
            to_edge[0].wait_recv()
            to_prev[0].wait_send()

        many = tot.at[k, pl.ds(0, count - 1)]
        pltpu.make_async_copy(many, many, tot_sem.at[k, 0]).wait()
        pltpu.make_async_copy(many, many, tot_sem.at[k, 1]).wait()

        both = jnp.sum(tot[k], axis=0)
        mean = jnp.sum(jnp.where(first_lane == 0, both, 0.0), axis=1, keepdims=True) / jnp.sum(
            jnp.where(first_lane == 1, both, 0.0), axis=1, keepdims=True)
        mine, theirs = contrib[k], pair[k]
        sums = jnp.where(on_diag, mine, theirs) + jnp.where(on_diag, theirs, mine)
        arrived = jnp.where(has_prev, edge_in[k], 0.0)
        if rows_dev > 1:
            arrived = jnp.concatenate([arrived, jnp.zeros((1, width - size), F32)], axis=1)
        sums = sums + arrived
        factor = jnp.where(mask[...] > 0, sums / mean, 1.0)
        bias_out[...] = bias_out[...] * factor
        inverse = 1.0 / factor
        next_sums = nxt[k, 0] + nxt[k, 1] + edge_out[k]
        next_inverse = 1.0 / jnp.where(next_mask[...] > 0, next_sums / mean, 1.0)
        next_inverse = jnp.where(has_next, next_inverse, 0.0)
        if rows_dev > 1:
            next_inverse = jnp.concatenate([inverse[:, size:], next_inverse], axis=1)
        u_out[...] = u_out[...] * inverse
        v_out[...] = v_out[...] * jnp.where(on_diag, inverse, next_inverse)

    for t, r in order:
        out_copy(t, r).wait()

    @pl.when(on_diag)
    def _():
        for t, r in order:
            piece(t, r, r * B).wait_send()

    @pl.when(off_diag)
    def _():
        for t, r in order:
            piece(t, r, 0).wait_send()


def local(n, held_tiles, placed, bin_mask, bias):
    rows_dev, size = held_tiles.shape[0], held_tiles.shape[2]
    strips, width, count = size // B, rows_dev * size, n * 2
    flags = jnp.broadcast_to(placed[:, None, None], (rows_dev, 1, B))
    vmem, anywhere = pl.BlockSpec(memory_space=pltpu.VMEM), pl.BlockSpec(memory_space=pl.ANY)
    wide = jax.ShapeDtypeStruct((1, width), F32)
    dma = pltpu.SemaphoreType.DMA
    tiles, u, v, bias_new = pl.pallas_call(
        functools.partial(kernel, n, rows_dev, size),
        out_shape=(jax.ShapeDtypeStruct((rows_dev, size, size), F32), wide, wide, wide),
        in_specs=[anywhere, vmem, vmem, vmem],
        out_specs=(anywhere, vmem, vmem, vmem),
        scratch_shapes=[
            pltpu.VMEM((rows_dev, size, size), F32),
            pltpu.VMEM((rows_dev, size, size), F32),
            pltpu.VMEM((1, width), F32),
            pltpu.VMEM((1, size), jnp.int32),
            pltpu.VMEM((1, width), F32),
            pltpu.VMEM((rows_dev, 8, size), F32),
            pltpu.VMEM((1, width), F32),
            pltpu.VMEM((ITERS, 1, width), F32),
            pltpu.VMEM((ITERS, 1, width), F32),
            pltpu.VMEM((ITERS, 1, size), F32),
            pltpu.VMEM((ITERS, 1, size), F32),
            pltpu.VMEM((ITERS, 2, 1, size), F32),
            pltpu.VMEM((ITERS, count, 1, B), F32),
            dma((rows_dev,)),
            dma((rows_dev, strips)),
            dma((rows_dev, strips)),
            dma((rows_dev, strips)),
            dma((2,)),
            dma((ITERS, 2)),
            dma((ITERS, 3)),
            dma((ITERS, 3)),
            dma((ITERS, 2)),
        ],
        compiler_params=pltpu.CompilerParams(collective_id=0, has_side_effects=True),
    )(held_tiles, flags, bin_mask.reshape(1, width), bias.reshape(1, width))
    u, v = u.reshape(rows_dev, 1, size, 1), v.reshape(rows_dev, 1, 1, size)
    return (tiles[:, None] * u) * v, bias_new.reshape(width)


def solution(mesh):
    specs = (P("bins", "diag", None, None), P("bins"), P("bins"), P("bins"))
    return jax.shard_map(
        functools.partial(local, mesh.shape["bins"]),
        mesh=mesh,
        in_specs=specs,
        out_specs=(P("bins", "diag", None, None), P("bins")),
        check_vma=False,
    )
```

time: 560 us -> 321 us (0.57)
  waiting for transfers between devices: 365 us -> 0 us
  Pallas kernels: 0 us -> 308 us
  blocking collectives: 87.9 us -> 0 us
  local copies, waits for them, and re-layouts: 49.6 us -> 2.43 us
  other arithmetic: 39.1 us -> 10.3 us
  starting transfers between devices: 13 us -> 0 us
    ppermute x6 -> x0, waiting for transfers between devices: 365 us -> none  [the longest x1 355 us: partner(): return lax.ppermute(value, axis, pairs)]
    pallas_call x0 -> x1, Pallas kernels: none -> 308 us  [local(): pl.pallas_call(functools.partial(kernel, n, rows_dev, size), out_shape=(j...]
    psum x4 -> x0, blocking collectives: 87.9 us -> none  [the longest x2 82.9 us: local(): lax.psum((jnp.sum(sums * live_home), jnp.sum(live_home)), 'bins')]
    reduce_sum x5 -> x0, other arithmetic: 30.7 us -> none  [the longest x2 28.8 us: local(): jnp.sum(scaled, axis=1) - jnp.where(on_diagonal, diagonal_terms, 0.0)]
    gather x2 -> x0, local copies, waits for them, and re-layouts: 26.6 us -> none  [local(): diagonal_terms = jnp.diagonal(scaled, axis1=1, axis2=2)]
    unnamed x9 -> x3, local copies, waits for them, and re-layouts: 22 us -> 0.6 us
    ppermute x6 -> x0, starting transfers between devices: 13 us -> none  [the longest x5 8.92 us: passed_along(): lax.ppermute(value, axis, [(source, source + steps) for source in range(f...]
    unnamed x1, other arithmetic: 0.02 us -> 7.54 us
  transfers between devices with their start and end apart: 6 -> 0, of which waited for: 6 -> 0; matrix products, arithmetic and copies ran while one was open for 1% -> 0% of each run, Pallas kernels for 0% -> 0%
where the time goes in v1:
time: 321 us
  Pallas kernels  308 us (96%)
  other arithmetic  10.3 us (3%)
    pallas_call x1, Pallas kernels, local(): pl.pallas_call(functools.partial(kernel, n, rows_dev, size), out_shape=(j...  308 us
    unnamed x1, other arithmetic  7.54 us

profile of v1, /device:TPU:0, one launch (start us, length us, event | category | flops | bytes accessed | tf_op | source)
XLA Modules:
  0.0 320.9 jit_solution(8451952308399924638)
XLA Ops:
  0.6 1.3 broadcast_in_dim.2.placed
  1.9 307.5 %shard_map.59 = (f32[2,1024,1024]{2,1,0:T(8,128)}, f32[1,2048]{1,0:T(1,128)}, f32[1,2048]{1,0:T(1,128)}, f32[1,2048]{1,0:T(1,128)}) custom-call(f32[2,1,1024,1024]{3,2,1,0:T(8,128)} %held.1, s32[2,1,128]{2,1,0:T(1,128)} %broadcast_in_dim.2.placed, s32[1,2048]{1,0:T(1,128)} %bitcast.8, f32[1,2048]{1,0:T(1,128)} %bitcast.9), custom_call_target="tpu_custom_call" | custom-call | tf_op jit(solution)/shard_map/pallas_call | solution.py:257
  309.4 0.5 broadcast.12
  309.9 1.4 reduce.7
  311.3 1.4 reduce.6
  312.7 0.0 copy-start
  312.7 7.5 %multiply_bitcast_fusion = f32[2,1,1024,1024]{3,2,1,0:T(8,128)} fusion(f32[2,1024,1024]{2,1,0:T(8,128)} %get-tuple-element.6, f32[2,1024]{1,0:T(2,128)S(1)} %mul.27, f32[2,1024]{1,0:T(2,128)S(1)} %mul.24), kind=kLoop, calls=%fused_computation | loop fusion | flops 4194304 | bytes 16793600
  320.3 0.0 copy-done
  320.3 0.6 copy.8
  (2 shorter events, 0.0 us)
Async XLA Ops:
  312.7 7.5 %copy-start = (f32[1,2048]{1,0:T(1,128)S(1)}, f32[1,2048]{1,0:T(1,128)}, u32[]{:S(2)}) copy-start(f32[1,2048]{1,0:T(1,128)} %get-tuple-element.9) | copy-start | bytes 24580

commit v2 on v1

--- a/solution.py
+++ b/solution.py
@@ -14,8 +14,8 @@
 
 
 def kernel(n, rows_dev, size, held, placed, mask, bias, tiles_out, u_out, v_out, bias_out,
-           home, recv, live_col, next_mask, row, col_acc, diag_vec, contrib, pair, edge_in, edge_out, nxt, tot,
-           in_sem, out_sem, send_sem, recv_sem, mask_sem, pair_sem, edge_sem, next_sem, tot_sem):
+           home, recv, live_col, next_mask, row, col_acc, diag_vec, contrib, pair, edge_in, edge_out, nxt, tot, fold_out, fold_in,
+           in_sem, out_sem, send_sem, recv_sem, mask_sem, pair_sem, edge_sem, next_sem, tot_sem, fold_sem):
     b, d = lax.axis_index("bins"), lax.axis_index("diag")
     count = n * 2
     me = b * 2 + d
@@ -58,15 +58,41 @@
 
     order = [(t, r) for t in range(rows_dev) for r in range(strips)]
 
+    def folds(t):
+        return pltpu.make_async_remote_copy(
+            fold_out.at[t], fold_in.at[t], fold_sem.at[t, 0], fold_sem.at[t, 1], device_id=partner, device_id_type=MESH)
+
+    line = lax.broadcasted_iota(jnp.int32, (B, B), 0)
+    lane = lax.broadcasted_iota(jnp.int32, (B, B), 1)
+
     @pl.when(on_diag)
     def _():
         for t, r in order:
-            piece(t, r, r * B).start()
+            if r < strips - 1:
+                piece(t, r, (r + 1) * B).start()
 
     @pl.when(off_diag)
     def _():
         for t, r in order:
             piece(t, r, 0).start()
+
+    for t in range(rows_dev):
+        loads[t].wait()
+
+    @pl.when(on_diag)
+    def _():
+        for t in range(rows_dev):
+            def fold(j, carry):
+                low, high = [pl.ds(pl.multiple_of((2 * j + i) * B, B), B) for i in range(2)]
+                even, odd = home[t, low, low], home[t, high, high]
+                fold_out[t, j, :B] = jnp.where(line <= lane, even, odd.T)
+                corner = jnp.sum(jnp.where(line == lane, odd, 0.0), axis=0, keepdims=True)
+                fold_out[t, j, B:] = jnp.broadcast_to(corner, (8, B))
+                return carry
+
+            lax.fori_loop(0, strips // 2, fold, 0)
+        for t in range(rows_dev):
+            folds(t).start()
 
     @pl.when(off_diag & has_next)
     def _():
@@ -81,11 +107,7 @@
     live_col[:, width - size:] = jnp.where(on_diag, live[:, width - size:], after)
     if rows_dev > 1:
         live_col[:, :width - size] = jnp.where(on_diag, live[:, :width - size], live[:, size:])
-    for t in range(rows_dev):
-        loads[t].wait()
     col_acc[...] = jnp.zeros_like(col_acc)
-    line = lax.broadcasted_iota(jnp.int32, (B, B), 0)
-    lane = lax.broadcasted_iota(jnp.int32, (B, B), 1)
     shift = jnp.where(on_diag, 0, -2 * size)
 
     def down(vector):
@@ -103,7 +125,19 @@
     for t, r in order:
         @pl.when(on_diag)
         def _():
-            piece(t, r, r * B).wait_recv()
+            if r == 0:
+                folds(t).wait_recv()
+
+                def unfold(j, carry):
+                    low, high = [pl.ds(pl.multiple_of((2 * j + i) * B, B), B) for i in range(2)]
+                    both = fold_in[t, j, :B]
+                    recv[t, low, low] = both
+                    recv[t, high, high] = jnp.where(line == lane, fold_in[t, j, B:B + 1], both.T)
+                    return carry
+
+                lax.fori_loop(0, strips // 2, unfold, 0)
+            if r < strips - 1:
+                piece(t, r, (r + 1) * B).wait_recv()
 
         @pl.when(off_diag)
         def _():
@@ -111,7 +145,7 @@
 
         spot = pl.ds(t * size + r * B, B)
         live_down = down(mask[:, spot].astype(F32))
-        moved = jnp.broadcast_to(placed[t], (B, B)) == 1
+        moved = jnp.full((B, B), placed[t]) == 1
 
         def first_pass(c, total):
             at = (t, pl.ds(r * B, B), lanes(c))
@@ -144,11 +178,13 @@
                     u_down = down(u_out[:, spot])
 
                     def later_pass(c, total):
-                        block = home[t, lanes(r), lanes(c)]
-                        col_acc[t, :, lanes(c)] += folded(block * u_down)
-                        return total + block * v_out[:, pl.ds(pl.multiple_of(t * size + c * B, B), B)]
-
-                    total = lax.fori_loop(0, strips, later_pass, jnp.zeros((B, B), F32))
+                        block = home[t, lanes(r), c * B:(c + 1) * B]
+                        col_acc[t, :, c * B:(c + 1) * B] += folded(block * u_down)
+                        return total + block * v_out[:, t * size + c * B:t * size + (c + 1) * B]
+
+                    total = jnp.zeros((B, B), F32)
+                    for c in range(strips):
+                        total = later_pass(c, total)
                     row[:, spot] = jnp.sum(total.T, axis=0, keepdims=True)
                     return carry
 
@@ -239,25 +275,36 @@
     @pl.when(on_diag)
     def _():
         for t, r in order:
-            piece(t, r, r * B).wait_send()
+            if r < strips - 1:
+                piece(t, r, (r + 1) * B).wait_send()
+        for t in range(rows_dev):
+            folds(t).wait_send()
 
     @pl.when(off_diag)
     def _():
         for t, r in order:
             piece(t, r, 0).wait_send()
+
+
+def scale(tall, tiles, u, v, out):
+    for r in range(tall // B):
+        spot = pl.ds(r * B, B)
+        u_down = jnp.broadcast_to(u[:, spot], (B, B)).T
+        for c in range(v.shape[1] // B):
+            across = pl.ds(c * B, B)
+            out[0, 0, spot, across] = tiles[0, spot, across] * u_down * v[:, across]
 
 
 def local(n, held_tiles, placed, bin_mask, bias):
     rows_dev, size = held_tiles.shape[0], held_tiles.shape[2]
     strips, width, count = size // B, rows_dev * size, n * 2
-    flags = jnp.broadcast_to(placed[:, None, None], (rows_dev, 1, B))
     vmem, anywhere = pl.BlockSpec(memory_space=pltpu.VMEM), pl.BlockSpec(memory_space=pl.ANY)
     wide = jax.ShapeDtypeStruct((1, width), F32)
     dma = pltpu.SemaphoreType.DMA
     tiles, u, v, bias_new = pl.pallas_call(
         functools.partial(kernel, n, rows_dev, size),
         out_shape=(jax.ShapeDtypeStruct((rows_dev, size, size), F32), wide, wide, wide),
-        in_specs=[anywhere, vmem, vmem, vmem],
+        in_specs=[anywhere, pl.BlockSpec(memory_space=pltpu.SMEM), vmem, vmem],
         out_specs=(anywhere, vmem, vmem, vmem),
         scratch_shapes=[
             pltpu.VMEM((rows_dev, size, size), F32),
@@ -273,6 +320,8 @@
             pltpu.VMEM((ITERS, 1, size), F32),
             pltpu.VMEM((ITERS, 2, 1, size), F32),
             pltpu.VMEM((ITERS, count, 1, B), F32),
+            pltpu.VMEM((rows_dev, strips // 2, B + 8, B), F32),
+            pltpu.VMEM((rows_dev, strips // 2, B + 8, B), F32),
             dma((rows_dev,)),
             dma((rows_dev, strips)),
             dma((rows_dev, strips)),
@@ -282,11 +331,23 @@
             dma((ITERS, 3)),
             dma((ITERS, 3)),
             dma((ITERS, 2)),
+            dma((rows_dev, 2)),
         ],
         compiler_params=pltpu.CompilerParams(collective_id=0, has_side_effects=True),
-    )(held_tiles, flags, bin_mask.reshape(1, width), bias.reshape(1, width))
-    u, v = u.reshape(rows_dev, 1, size, 1), v.reshape(rows_dev, 1, 1, size)
-    return (tiles[:, None] * u) * v, bias_new.reshape(width)
+    )(held_tiles, placed, bin_mask.reshape(1, width), bias.reshape(1, width))
+    tall = 4 * B
+    balanced = pl.pallas_call(
+        functools.partial(scale, tall),
+        grid=(rows_dev, size // tall),
+        out_shape=jax.ShapeDtypeStruct((rows_dev, 1, size, size), F32),
+        in_specs=[
+            pl.BlockSpec((1, tall, size), lambda t, s: (t, s, 0)),
+            pl.BlockSpec((1, tall), lambda t, s: (0, t * (size // tall) + s)),
+            pl.BlockSpec((1, size), lambda t, s: (0, t)),
+        ],
+        out_specs=pl.BlockSpec((1, 1, tall, size), lambda t, s: (t, 0, s, 0)),
+    )(tiles, u, v)
+    return balanced, bias_new.reshape(width)
 
 
 def solution(mesh):

time: 321 us -> 302 us (0.941)
  other arithmetic: 10.3 us -> 0 us
  Pallas kernels: 308 us -> 301 us
    pallas_call x1, Pallas kernels: 308 us -> 293 us  [local(): pl.pallas_call(functools.partial(kernel, n, rows_dev, size), out_shape=(j...]
    unnamed x1 -> x0, other arithmetic: 7.54 us -> none
    pallas_call x0 -> x1, Pallas kernels: none -> 7.33 us  [local(): pl.pallas_call(functools.partial(scale, tall), grid=(rows_dev, size // ta...]
where the time goes in v2:
time: 302 us
  Pallas kernels  301 us (100%)
    pallas_call x1, Pallas kernels, local(): pl.pallas_call(functools.partial(kernel, n, rows_dev, size), out_shape=(j...  293 us
    pallas_call x1, Pallas kernels, local(): pl.pallas_call(functools.partial(scale, tall), grid=(rows_dev, size // ta...  7.33 us

profile of v2, /device:TPU:0, one launch (start us, length us, event | category | flops | bytes accessed | tf_op | source)
XLA Modules:
  0.0 302.0 jit_solution(13400599657224619205)
XLA Ops:
  0.6 293.4 %shard_map.59 = (f32[2,1024,1024]{2,1,0:T(8,128)}, f32[1,2048]{1,0:T(1,128)}, f32[1,2048]{1,0:T(1,128)}, f32[1,2048]{1,0:T(1,128)}) custom-call(f32[2,1,1024,1024]{3,2,1,0:T(8,128)} %held.1, s32[2]{0:T(128)} %placed.1, s32[1,2048]{1,0:T(1,128)} %bitcast.4, f32[1,2048]{1,0:T(1,128)} %bitcast.5), custom_call_target="tpu_custom_call" | custom-call | tf_op jit(solution)/shard_map/pallas_call | solution.py:304
  294.0 0.0 copy-start
  294.0 7.3 %shard_map.60 = f32[2,1,1024,1024]{3,2,1,0:T(8,128)} custom-call(f32[2,1024,1024]{2,1,0:T(8,128)} %get-tuple-element.6.tiles, f32[1,2048]{1,0:T(1,128)} %get-tuple-element.7.u, f32[1,2048]{1,0:T(1,128)} %get-tuple-element.8.v), custom_call_target="tpu_custom_call" | custom-call | tf_op jit(solution)/shard_map/pallas_call | solution.py:339
  301.4 0.0 copy-done
  301.4 0.6 copy.7
Async XLA Ops:
  294.0 7.3 %copy-start = (f32[1,2048]{1,0:T(1,128)S(1)}, f32[1,2048]{1,0:T(1,128)}, u32[]{:S(2)}) copy-start(f32[1,2048]{1,0:T(1,128)} %get-tuple-element.9) | copy-start | bytes 24580

commit v3 on v2

--- a/solution.py
+++ b/solution.py
@@ -14,7 +14,7 @@
 
 
 def kernel(n, rows_dev, size, held, placed, mask, bias, tiles_out, u_out, v_out, bias_out,
-           home, recv, live_col, next_mask, row, col_acc, diag_vec, contrib, pair, edge_in, edge_out, nxt, tot, fold_out, fold_in,
+           home, recv, live_col, next_mask, row, col_acc, diag_vec, contrib, pair, edge_in, edge_out, nxt, tot, fold_out, fold_in, sums_now,
            in_sem, out_sem, send_sem, recv_sem, mask_sem, pair_sem, edge_sem, next_sem, tot_sem, fold_sem):
     b, d = lax.axis_index("bins"), lax.axis_index("diag")
     count = n * 2
@@ -169,6 +169,18 @@
     bias_out[...] = bias[...]
     first_lane = lax.broadcasted_iota(jnp.int32, (1, B), 1)
 
+    def settle(k):
+        many = tot.at[k, pl.ds(0, count - 1)]
+        pltpu.make_async_copy(many, many, tot_sem.at[k, 0]).wait()
+        pltpu.make_async_copy(many, many, tot_sem.at[k, 1]).wait()
+        both = jnp.sum(tot[k], axis=0)
+        mean = jnp.sum(jnp.where(first_lane == 0, both, 0.0), axis=1, keepdims=True) / jnp.sum(
+            jnp.where(first_lane == 1, both, 0.0), axis=1, keepdims=True)
+        bias_out[...] = bias_out[...] * jnp.where(mask[...] > 0, sums_now[...] / mean, 1.0)
+        u_out[...] = u_out[...] * jnp.where(mask[...] > 0, mean, 1.0)
+        v_out[...] = v_out[...] * jnp.where(live_col[...] > 0, mean, 1.0)
+        return mean
+
     for k in range(ITERS):
         if k > 0:
             col_acc[...] = jnp.zeros_like(col_acc)
@@ -196,6 +208,9 @@
         moved_cols = jnp.concatenate([zero, cols[:, :width - size]], axis=1)
         mine = rows + jnp.where(on_diag, cols - corner, moved_cols)
         edge = jnp.where(on_diag, 0.0, cols[:, width - size:])
+        if k > 0:
+            mean = settle(k - 1)
+            mine, edge = (jnp.where(value != 0, value * mean * mean, 0.0) for value in (mine, edge))
         contrib[k] = mine
         edge_out[k] = edge
         partial = jnp.sum(mine) + jnp.sum(edge)
@@ -229,8 +244,8 @@
             def _():
                 to_prev[i].start()
 
+        to_pair.start()
         lax.fori_loop(1, count, tot_start, 0)
-        to_pair.start()
         to_pair.wait()
 
         @pl.when(off_diag & has_next)
@@ -245,30 +260,24 @@
             to_edge[0].wait_recv()
             to_prev[0].wait_send()
 
-        many = tot.at[k, pl.ds(0, count - 1)]
-        pltpu.make_async_copy(many, many, tot_sem.at[k, 0]).wait()
-        pltpu.make_async_copy(many, many, tot_sem.at[k, 1]).wait()
-
-        both = jnp.sum(tot[k], axis=0)
-        mean = jnp.sum(jnp.where(first_lane == 0, both, 0.0), axis=1, keepdims=True) / jnp.sum(
-            jnp.where(first_lane == 1, both, 0.0), axis=1, keepdims=True)
         mine, theirs = contrib[k], pair[k]
         sums = jnp.where(on_diag, mine, theirs) + jnp.where(on_diag, theirs, mine)
         arrived = jnp.where(has_prev, edge_in[k], 0.0)
         if rows_dev > 1:
             arrived = jnp.concatenate([arrived, jnp.zeros((1, width - size), F32)], axis=1)
         sums = sums + arrived
-        factor = jnp.where(mask[...] > 0, sums / mean, 1.0)
-        bias_out[...] = bias_out[...] * factor
-        inverse = 1.0 / factor
+        sums_now[...] = sums
+        inverse = 1.0 / jnp.where(mask[...] > 0, sums, 1.0)
         next_sums = nxt[k, 0] + nxt[k, 1] + edge_out[k]
-        next_inverse = 1.0 / jnp.where(next_mask[...] > 0, next_sums / mean, 1.0)
+        next_inverse = 1.0 / jnp.where(next_mask[...] > 0, next_sums, 1.0)
         next_inverse = jnp.where(has_next, next_inverse, 0.0)
         if rows_dev > 1:
             next_inverse = jnp.concatenate([inverse[:, size:], next_inverse], axis=1)
         u_out[...] = u_out[...] * inverse
         v_out[...] = v_out[...] * jnp.where(on_diag, inverse, next_inverse)
 
+    settle(ITERS - 1)
+
     for t, r in order:
         out_copy(t, r).wait()
 
@@ -286,7 +295,8 @@
             piece(t, r, 0).wait_send()
 
 
-def scale(tall, tiles, u, v, out):
+def scale(tall, tiles, u, v, bias, out, bias_out):
+    bias_out[...] = bias[...]
     for r in range(tall // B):
         spot = pl.ds(r * B, B)
         u_down = jnp.broadcast_to(u[:, spot], (B, B)).T
@@ -322,6 +332,7 @@
             pltpu.VMEM((ITERS, count, 1, B), F32),
             pltpu.VMEM((rows_dev, strips // 2, B + 8, B), F32),
             pltpu.VMEM((rows_dev, strips // 2, B + 8, B), F32),
+            pltpu.VMEM((1, width), F32),
             dma((rows_dev,)),
             dma((rows_dev, strips)),
             dma((rows_dev, strips)),
@@ -335,18 +346,19 @@
         ],
         compiler_params=pltpu.CompilerParams(collective_id=0, has_side_effects=True),
     )(held_tiles, placed, bin_mask.reshape(1, width), bias.reshape(1, width))
-    tall = 4 * B
-    balanced = pl.pallas_call(
+    tall = 2 * B
+    balanced, bias_new = pl.pallas_call(
         functools.partial(scale, tall),
         grid=(rows_dev, size // tall),
-        out_shape=jax.ShapeDtypeStruct((rows_dev, 1, size, size), F32),
+        out_shape=(jax.ShapeDtypeStruct((rows_dev, 1, size, size), F32), wide),
         in_specs=[
             pl.BlockSpec((1, tall, size), lambda t, s: (t, s, 0)),
             pl.BlockSpec((1, tall), lambda t, s: (0, t * (size // tall) + s)),
             pl.BlockSpec((1, size), lambda t, s: (0, t)),
+            pl.BlockSpec((1, width), lambda t, s: (0, 0)),
         ],
-        out_specs=pl.BlockSpec((1, 1, tall, size), lambda t, s: (t, 0, s, 0)),
-    )(tiles, u, v)
+        out_specs=(pl.BlockSpec((1, 1, tall, size), lambda t, s: (t, 0, s, 0)), pl.BlockSpec((1, width), lambda t, s: (0, 0))),
+    )(tiles, u, v, bias_new)
     return balanced, bias_new.reshape(width)
 
 

time: 302 us -> 302 us (level)
  no operation moved by 1% of the time
where the time goes in v3:
time: 302 us; the launch traced here: 301 us
  Pallas kernels  301 us (100%)
    pallas_call x1, Pallas kernels, local(): pl.pallas_call(functools.partial(kernel, n, rows_dev, size), out_shape=(j...  291 us
    pallas_call x1, Pallas kernels, local(): pl.pallas_call(functools.partial(scale, tall), grid=(rows_dev, size // ta...  9.32 us

profile of v3, /device:TPU:0, one launch (start us, length us, event | category | flops | bytes accessed | tf_op | source)
XLA Modules:
  0.0 301.3 jit_solution(13221631327755244296)
XLA Ops:
  0.6 291.3 %shard_map.59 = (f32[2,1024,1024]{2,1,0:T(8,128)}, f32[1,2048]{1,0:T(1,128)}, f32[1,2048]{1,0:T(1,128)}, f32[1,2048]{1,0:T(1,128)}) custom-call(f32[2,1,1024,1024]{3,2,1,0:T(8,128)} %held.1, s32[2]{0:T(128)} %placed.1, s32[1,2048]{1,0:T(1,128)} %bitcast.3, f32[1,2048]{1,0:T(1,128)} %bitcast.4), custom_call_target="tpu_custom_call" | custom-call | tf_op jit(solution)/shard_map/pallas_call | solution.py:314
  292.0 9.3 %shard_map.60 = (f32[2,1,1024,1024]{3,2,1,0:T(8,128)}, f32[1,2048]{1,0:T(1,128)}) custom-call(f32[2,1024,1024]{2,1,0:T(8,128)} %get-tuple-element.8.tiles, f32[1,2048]{1,0:T(1,128)} %get-tuple-element.9.u, f32[1,2048]{1,0:T(1,128)} %get-tuple-element.10.v, f32[1,2048]{1,0:T(1,128)} %get-tuple-element.11.bias), custom_call_target="tpu_custom_call" | custom-call | tf_op jit(solution)/shard_map/pallas_call | solution.py:350
